TPU v7x, 32 devices: a whole 2x2x4 slice. The times are simulated.
32 devices in a mesh: wide: 8 (over y, x, core), narrow: 4 (over z).
Axes of the slice: x: 2, y: 2, z: 4, core: 2. Of those that a mesh axis runs over, the one named last changes fastest.
Arguments:
- tokens: bfloat16 [4096, 4096], P(('wide', 'narrow')), may hold values from -6 to 6
- cotangent: bfloat16 [4096, 4096], P(('wide', 'narrow')), may hold values from -6 to 6
- weights: bfloat16 [32, 6, 256, 256], P(('wide', 'narrow')), may hold values from -0.1875 to 0.1875
- block_index: int32 [32, 6], P(('wide', 'narrow')), may hold values from 0 to 15, as said below
- block_counts: int32 [32], P(('wide', 'narrow')), may hold values from 1 to 6, as said below
Outputs:
- mixed: bfloat16 [4096, 4096], P(('wide', 'narrow'))
- grad_tokens: bfloat16 [4096, 4096], P(('wide', 'narrow'))
Inputs may be any that keep to these rules, and one draw needn't show every extreme that they name: `block_index`: each row lists 6 distinct blocks. `block_counts`: slots at or beyond a row's count are unused.
All inputs are finite; a program needn't handle non-finite values.
Results may differ from a plain program's by a relative error of at most 0.008.
Values may be sent and summed in bfloat16 or wider, within the bound.
No kernel may reach another device: no remote copies, remote signals or barrier semaphores. Data moves between devices by JAX's collectives and lax.ppermute only.
A program may use at most 192 MiB of HBM per device.

v0:
```python
import jax
import jax.numpy as jnp
from jax import lax
from jax.sharding import PartitionSpec as P


def from_root(block, axis, source):
    block = jnp.where(lax.axis_index(axis) == source, block, jnp.zeros_like(block))
    return lax.psum(block, axis)


def activate(values):
    return jax.nn.gelu(values, approximate=True)


def body(tokens, cotangent, weights, block_index, block_counts):
    rows_tok, rows_cot = (
        lax.all_gather(tokens, "narrow", axis=0, tiled=True),
        lax.all_gather(cotangent, "narrow", axis=0, tiled=True),
    )
    wide_count = lax.axis_size("wide")

    def receive(section_num, buffers):
        received = (
            from_root(weights, "wide", section_num),
            from_root(block_index, "wide", section_num),
            from_root(block_counts, "wide", section_num),
        )
        return tuple(
            (
                lax.dynamic_update_index_in_dim(buffer, piece[0], section_num, 0)
                for buffer, piece in zip(buffers, received)
            )
        )

    initial = (
        jnp.zeros((wide_count,) + weights.shape[1:], weights.dtype),
        jnp.zeros((wide_count, block_index.shape[1]), jnp.int32),
        jnp.zeros((wide_count,), jnp.int32),
    )
    blocks_all, indices_all, counts_all = lax.fori_loop(0, wide_count, receive, initial)
    half_wide = wide_count // 2
    num_slots = blocks_all.shape[1]
    block_width = blocks_all.shape[2]
    live_mask = (jnp.arange(num_slots)[None, :] < counts_all[:, None]).astype(jnp.bfloat16)
    kept_blocks = blocks_all * live_mask[:, :, None, None]
    num_rows = rows_tok.shape[0]
    num_blocks = rows_tok.shape[1] // block_width
    tok_blocks = rows_tok.reshape(num_rows, num_blocks, block_width)
    cot_blocks = rows_cot.reshape(num_rows, num_blocks, block_width)
    panel_items = (
        kept_blocks[:half_wide],
        indices_all[:half_wide],
        kept_blocks[half_wide:],
        indices_all[half_wide:],
    )
    zeros_acc = jnp.zeros((num_rows, num_blocks, block_width), jnp.float32)

    def forward(running, panel_item):
        w_first, idx_first, w_second, idx_second = panel_item
        picked = jnp.take(tok_blocks, idx_first, axis=1)
        pre_act = jnp.einsum("tjd,jdh->th", picked, w_first, preferred_element_type=jnp.float32)
        act_out = activate(pre_act).astype(jnp.bfloat16)
        running = running.at[:, idx_second].add(
            jnp.einsum("th,jhd->tjd", act_out, w_second, preferred_element_type=jnp.float32)
        )
        return (running, pre_act)

    def backward(running, panel_item):
        w_first, idx_first, w_second, idx_second, pre_act = panel_item
        cot_picked = jnp.take(cot_blocks, idx_second, axis=1)
        grad_act = jnp.einsum(
            "tjd,jhd->th", cot_picked, w_second, preferred_element_type=jnp.float32
        )
        grad_pre = jax.vjp(activate, pre_act)[1](grad_act)[0].astype(jnp.bfloat16)
        running = running.at[:, idx_first].add(
            jnp.einsum("th,jdh->tjd", grad_pre, w_first, preferred_element_type=jnp.float32)
        )
        return (running, None)

    out_acc, pre_stack = lax.scan(forward, zeros_acc, panel_items)
    grad_acc, _ = lax.scan(backward, zeros_acc, panel_items + (pre_stack,))
    out_part = out_acc.reshape(num_rows, -1).astype(jnp.bfloat16)
    grad_part = grad_acc.reshape(num_rows, -1).astype(jnp.bfloat16)
    mixed, grad_tokens = (
        lax.psum_scatter(out_part, "narrow", scatter_dimension=0, tiled=True).astype(jnp.float32),
        lax.psum_scatter(grad_part, "narrow", scatter_dimension=0, tiled=True).astype(jnp.float32),
    )
    return (mixed.astype(jnp.bfloat16), grad_tokens.astype(jnp.bfloat16))


def solution(mesh):
    placed = (
        P(("wide", "narrow"), None),
        P(("wide", "narrow"), None),
        P(("wide", "narrow"), None, None, None),
        P(("wide", "narrow"), None),
        P(("wide", "narrow")),
    )
    return jax.shard_map(
        body,
        mesh=mesh,
        in_specs=placed,
        out_specs=(P(("wide", "narrow"), None), P(("wide", "narrow"), None)),
        check_vma=False,
    )
```

profile of v0, /device:TPU:0, one launch (start us, length us, event | category | flops | bytes accessed | tf_op | source)
XLA Modules:
  0.0 832.8 jit_solution(13676505129722302704)
XLA Ops:
  8.0 2.3 copy.13
  10.3 494.1 %while.41 = (s32[]{:T(128)}, bf16[8,6,256,256]{3,2,1,0:T(8,128)(2,1)}, s32[8,6]{1,0:T(8,128)S(1)}, s32[8]{0:T(128)S(1)}, bf16[1,6,256,256]{3,2,1,0:T(8,128)(2,1)...) while((s32[]{:T(128)}, ...), condition=%wide.region_4.5_spmd, body=%wide.region_0.4_spmd.sunk | while | flops 786452 | bytes 7864713 | solution.py:41
  10.3 2.2 broadcast_select_fusion.4
  13.8 8.2 all-reduce.2
  22.7 50.4 %all-reduce.5.cloned.1.call-done = bf16[1,6,256,256]{3,2,1,0:T(8,128)(2,1)} async-done(((bf16[1,6,256,256]{3,2,1,0:T(8,128)(2,1)}), bf16[1,6,256,256]{3,2,1,0:T(8,128)(2,1)}) %all-reduce.5.cloned.1.call-update) | async-done | bytes 786448 | tf_op jit(solution)/shard_map/while/body/eval_jaxpr/psum | solution.py:9
  73.1 2.1 constant_dynamic-update-slice_fusion.2
  76.8 7.2 all-reduce.2
  84.7 49.8 %all-reduce.5.cloned.1.call-done = bf16[1,6,256,256]{3,2,1,0:T(8,128)(2,1)} async-done(((bf16[1,6,256,256]{3,2,1,0:T(8,128)(2,1)}), bf16[1,6,256,256]{3,2,1,0:T(8,128)(2,1)}) %all-reduce.5.cloned.1.call-update) | async-done | bytes 786448 | tf_op jit(solution)/shard_map/while/body/eval_jaxpr/psum | solution.py:9
  134.6 2.1 constant_dynamic-update-slice_fusion.2
  138.3 7.8 all-reduce.2
  146.8 49.1 %all-reduce.5.cloned.1.call-done = bf16[1,6,256,256]{3,2,1,0:T(8,128)(2,1)} async-done(((bf16[1,6,256,256]{3,2,1,0:T(8,128)(2,1)}), bf16[1,6,256,256]{3,2,1,0:T(8,128)(2,1)}) %all-reduce.5.cloned.1.call-update) | async-done | bytes 786448 | tf_op jit(solution)/shard_map/while/body/eval_jaxpr/psum | solution.py:9
  196.0 2.1 constant_dynamic-update-slice_fusion.2
  199.7 7.2 all-reduce.2
  207.6 49.5 %all-reduce.5.cloned.1.call-done = bf16[1,6,256,256]{3,2,1,0:T(8,128)(2,1)} async-done(((bf16[1,6,256,256]{3,2,1,0:T(8,128)(2,1)}), bf16[1,6,256,256]{3,2,1,0:T(8,128)(2,1)}) %all-reduce.5.cloned.1.call-update) | async-done | bytes 786448 | tf_op jit(solution)/shard_map/while/body/eval_jaxpr/psum | solution.py:9
  260.8 8.9 %all-reduce.2 = (s32[1,6]{1,0:T(1,128)S(1)}, s32[1]{0:T(128)}) all-reduce(s32[1,6]{1,0:T(1,128)S(1)} %broadcast_select_fusion.5, s32[1]{0:T(128)S(6)} %select_n.151), channel_id=1, replica_groups=mesh['wide'=8,'narrow'=4] {'wide'}, use_global_device_ids=true, to_apply=%region_2.2 | all-reduce | flops 7 | bytes 56 | tf_op jit(solution)/shard_map/while/body/eval_jaxpr/psum | solution.py:9
  270.5 47.7 %all-reduce.5.cloned.1.call-done = bf16[1,6,256,256]{3,2,1,0:T(8,128)(2,1)} async-done(((bf16[1,6,256,256]{3,2,1,0:T(8,128)(2,1)}), bf16[1,6,256,256]{3,2,1,0:T(8,128)(2,1)}) %all-reduce.5.cloned.1.call-update) | async-done | bytes 786448 | tf_op jit(solution)/shard_map/while/body/eval_jaxpr/psum | solution.py:9
  318.2 2.1 constant_dynamic-update-slice_fusion.2
  322.0 7.2 all-reduce.2
  329.9 49.5 %all-reduce.5.cloned.1.call-done = bf16[1,6,256,256]{3,2,1,0:T(8,128)(2,1)} async-done(((bf16[1,6,256,256]{3,2,1,0:T(8,128)(2,1)}), bf16[1,6,256,256]{3,2,1,0:T(8,128)(2,1)}) %all-reduce.5.cloned.1.call-update) | async-done | bytes 786448 | tf_op jit(solution)/shard_map/while/body/eval_jaxpr/psum | solution.py:9
  379.4 2.1 constant_dynamic-update-slice_fusion.2
  383.1 8.5 %all-reduce.2 = (s32[1,6]{1,0:T(1,128)S(1)}, s32[1]{0:T(128)}) all-reduce(s32[1,6]{1,0:T(1,128)S(1)} %broadcast_select_fusion.5, s32[1]{0:T(128)S(6)} %select_n.151), channel_id=1, replica_groups=mesh['wide'=8,'narrow'=4] {'wide'}, use_global_device_ids=true, to_apply=%region_2.2 | all-reduce | flops 7 | bytes 56 | tf_op jit(solution)/shard_map/while/body/eval_jaxpr/psum | solution.py:9
  392.4 48.5 %all-reduce.5.cloned.1.call-done = bf16[1,6,256,256]{3,2,1,0:T(8,128)(2,1)} async-done(((bf16[1,6,256,256]{3,2,1,0:T(8,128)(2,1)}), bf16[1,6,256,256]{3,2,1,0:T(8,128)(2,1)}) %all-reduce.5.cloned.1.call-update) | async-done | bytes 786448 | tf_op jit(solution)/shard_map/while/body/eval_jaxpr/psum | solution.py:9
  444.5 7.2 all-reduce.2
  452.4 49.8 %all-reduce.5.cloned.1.call-done = bf16[1,6,256,256]{3,2,1,0:T(8,128)(2,1)} async-done(((bf16[1,6,256,256]{3,2,1,0:T(8,128)(2,1)}), bf16[1,6,256,256]{3,2,1,0:T(8,128)(2,1)}) %all-reduce.5.cloned.1.call-update) | async-done | bytes 786448 | tf_op jit(solution)/shard_map/while/body/eval_jaxpr/psum | solution.py:9
  502.3 2.1 constant_dynamic-update-slice_fusion.2
  506.5 3.3 broadcast_multiply_fusion
  509.7 3.1 fusion.90
  512.8 73.8 %all-gather.3.cloned.1.call-done = bf16[512,4096]{0,1:T(8,128)(2,1)} async-done(((bf16[128,4096]{0,1:T(8,128)(2,1)}), bf16[512,4096]{0,1:T(8,128)(2,1)}) %all-gather.3.cloned.1.call-update) | async-done | bytes 4194320 | tf_op jit(solution)/shard_map/all_gather | solution.py:18
  586.6 6.4 copy.14
  593.1 4.1 broadcast_in_dim.36.clone
  597.1 59.3 %while.42 = (s32[]{:T(128)}, f32[512,16,256]{2,0,1:T(8,128)}, f32[4,512,256]{2,1,0:T(8,128)}, s32[4,6]{1,0:T(4,128)S(1)}, s32[4,6]{1,0:T(4,128)S(1)}, /*index=5*...) while((s32[]{:T(128)}, f32[512,16,256]{2,0,1:T(8,128)}, ...), condition=%wide.region_7.9_spmd, body=%wide.region_5.8_spmd.sunk | while | flops 808059968 | bytes 20452644 | solution.py:81
  597.2 2.9 gather_fusion
  600.1 2.6 bitcast_dynamic-update-slice_fusion.2
  604.4 7.6 scatter_fusion
  612.0 2.9 gather_fusion
  614.9 2.6 bitcast_dynamic-update-slice_fusion.2
  619.2 7.6 scatter_fusion
  626.9 2.9 gather_fusion
  629.7 2.6 bitcast_dynamic-update-slice_fusion.2
  634.0 7.6 scatter_fusion
  641.7 2.8 gather_fusion
  644.5 2.5 bitcast_dynamic-update-slice_fusion.2
  648.8 7.6 scatter_fusion
  656.5 3.9 convert_bitcast_fusion.1
  660.4 2.5 copy.19
  662.9 4.3 all-gather.5.cloned.1.call-done
  667.3 6.3 copy.17
  673.6 4.1 broadcast_in_dim.36
  677.7 63.0 %while.43 = (s32[]{:T(128)}, f32[512,16,256]{2,0,1:T(8,128)}, s32[4,6]{1,0:T(4,128)S(1)}, s32[4,6]{1,0:T(4,128)S(1)}, bf16[512,16,256]{2,0,1:T(8,128)(2,1)}, /*i...) while((s32[]{:T(128)}, f32[512,16,256]{2,0,1:T(8,128)}, ...), condition=%wide.region_11.13_spmd, body=%wide.region_9.12_spmd.sunk | while | flops 809501760 | bytes 19404576 | solution.py:82
  677.7 4.1 gather_fusion.1
  681.8 4.0 convolution_bitcast_fusion.5
  685.8 7.6 scatter_fusion.1
  693.5 4.2 gather_fusion.1
  697.7 4.0 convolution_bitcast_fusion.5
  701.6 7.6 scatter_fusion.1
  709.3 4.1 gather_fusion.1
  713.4 4.1 convolution_bitcast_fusion.5
  717.4 7.6 scatter_fusion.1
  725.1 4.1 gather_fusion.1
  729.2 4.0 convolution_bitcast_fusion.5
  733.1 7.6 scatter_fusion.1
  740.7 3.9 convert_bitcast_fusion
  744.6 2.5 copy.20
  747.2 78.0 %reduce-scatter.5.cloned.1.call-done = bf16[128,4096]{1,0:T(8,128)(2,1)} async-done(((bf16[512,4096]{1,0:T(8,128)(2,1)}), bf16[128,4096]{1,0:T(8,128)(2,1)}) %reduce-scatter.5.cloned.1.call-update) | async-done | bytes 1048592 | tf_op jit(solution)/shard_map/reduce_scatter | solution.py:87
  (95 shorter events, 26.9 us)
Async XLA Ops:
  10.3 494.7 %copy-start = (bf16[128,4096]{1,0:T(8,128)(2,1)S(1)}, bf16[128,4096]{1,0:T(8,128)(2,1)}, u32[]{:S(2)}) copy-start(bf16[128,4096]{1,0:T(8,128)(2,1)} %param.14) | copy-start | bytes 3145732
  10.3 62.8 %all-reduce.5.cloned.1.call-start = ((), (), s32[]{:S(2)}) async-start(), calls=%async_computation.6 | async-start | bytes 1572864 | tf_op jit(solution)/shard_map/while/body/eval_jaxpr/psum | solution.py:9
  75.2 59.4 %all-reduce.5.cloned.1.call-start = ((), (), s32[]{:S(2)}) async-start(), calls=%async_computation.6 | async-start | bytes 1572864 | tf_op jit(solution)/shard_map/while/body/eval_jaxpr/psum | solution.py:9
  136.6 59.4 %all-reduce.5.cloned.1.call-start = ((), (), s32[]{:S(2)}) async-start(), calls=%async_computation.6 | async-start | bytes 1572864 | tf_op jit(solution)/shard_map/while/body/eval_jaxpr/psum | solution.py:9
  198.1 59.1 %all-reduce.5.cloned.1.call-start = ((), (), s32[]{:S(2)}) async-start(), calls=%async_computation.6 | async-start | bytes 1572864 | tf_op jit(solution)/shard_map/while/body/eval_jaxpr/psum | solution.py:9
  259.2 59.1 %all-reduce.5.cloned.1.call-start = ((), (), s32[]{:S(2)}) async-start(), calls=%async_computation.6 | async-start | bytes 1572864 | tf_op jit(solution)/shard_map/while/body/eval_jaxpr/psum | solution.py:9
  320.3 59.1 %all-reduce.5.cloned.1.call-start = ((), (), s32[]{:S(2)}) async-start(), calls=%async_computation.6 | async-start | bytes 1572864 | tf_op jit(solution)/shard_map/while/body/eval_jaxpr/psum | solution.py:9
  381.5 59.4 %all-reduce.5.cloned.1.call-start = ((), (), s32[]{:S(2)}) async-start(), calls=%async_computation.6 | async-start | bytes 1572864 | tf_op jit(solution)/shard_map/while/body/eval_jaxpr/psum | solution.py:9
  442.9 59.4 %all-reduce.5.cloned.1.call-start = ((), (), s32[]{:S(2)}) async-start(), calls=%async_computation.6 | async-start | bytes 1572864 | tf_op jit(solution)/shard_map/while/body/eval_jaxpr/psum | solution.py:9
  504.4 82.3 %all-gather.3.cloned.1.call-start = ((), (), s32[]{:S(2)}) async-start(), calls=%async_computation.2 | async-start | bytes 5242880 | tf_op jit(solution)/shard_map/all_gather | solution.py:18
  504.9 162.3 %all-gather.5.cloned.1.call-start = ((), (), s32[]{:S(2)}) async-start(), calls=%async_computation.4 | async-start | bytes 5242880 | tf_op jit(solution)/shard_map/all_gather | solution.py:19
  506.3 240.8 %reduce-scatter.3.cloned.1.call-start = ((), (), s32[]{:S(2)}) async-start(), calls=%async_computation.3 | async-start | bytes 5242880 | tf_op jit(solution)/shard_map/reduce_scatter | solution.py:86
  662.9 162.3 %reduce-scatter.5.cloned.1.call-start = ((), (), s32[]{:S(2)}) async-start(), calls=%async_computation.5 | async-start | bytes 5242880 | tf_op jit(solution)/shard_map/reduce_scatter | solution.py:87
Sparse Core Ops, SparseCore 0:
  14.8 58.2 all-reduce.4
  79.7 54.7 all-reduce.4
  141.2 54.7 all-reduce.4
  202.3 54.7 all-reduce.4
  263.4 54.7 all-reduce.4
  324.6 54.7 all-reduce.4
  386.0 54.7 all-reduce.4
  447.4 54.7 all-reduce.4
Sparse Core Ops, SparseCore 1:
  507.0 79.6 all-gather.2
  588.6 78.6 all-gather.4
  670.0 74.9 reduce-scatter.2
  748.0 77.2 reduce-scatter.4
where the time goes:
time: 835 us; the launch traced here: 833 us
  waiting for transfers between devices  551 us (66%)
  local copies, waits for them, and re-layouts  83.3 us (10%)
  other arithmetic  81.7 us (10%)
  blocking collectives  62.1 us (7%)
  matrix products  33.1 us (4%)
  between operations  15.7 us (2%)
    psum x8, waiting for transfers between devices, from_root(): return lax.psum(block, axis)  394 us
    reduce_scatter x1, waiting for transfers between devices, body(): lax.psum_scatter(grad_part, 'narrow', scatter_dimension=0, tiled=True)  78 us
    all_gather x1, waiting for transfers between devices, body(): lax.all_gather(tokens, 'narrow', axis=0, tiled=True)  73.8 us
    psum x8, blocking collectives, from_root(): return lax.psum(block, axis)  62.1 us
    scatter-add x4, other arithmetic, forward(): running.at[:, idx_second]  30.5 us
    scatter-add x4, other arithmetic, backward(): running.at[:, idx_first]  30.5 us
    dynamic_update_slice x24, local copies, waits for them, and re-layouts, receive(): lax.dynamic_update_index_in_dim(buffer, piece[0], section_num, 0)  22.7 us
  transfers between devices with their start and end apart: 12, of which 11 were waited for; matrix products, arithmetic and copies ran while one was open for 20% of the time, Pallas kernels for 0%

commit v1 on v0

--- a/solution.py
+++ b/solution.py
@@ -6,7 +6,7 @@
 
 def from_root(block, axis, source):
     block = jnp.where(lax.axis_index(axis) == source, block, jnp.zeros_like(block))
-    return lax.psum(block, axis)
+    return jnp.sum(lax.all_gather(block, axis), axis=0)
 
 
 def activate(values):

time: 835 us -> 773 us (0.926)
  waiting for transfers between devices: 551 us -> 374 us
  blocking collectives: 62.1 us -> 133 us
  other arithmetic: 81.7 us -> 129 us
    psum x8 -> x0, waiting for transfers between devices: 394 us -> none  [from_root(): return lax.psum(block, axis)]
    all_gather x0 -> x8, waiting for transfers between devices: none -> 216 us  [from_root(): return jnp.sum(lax.all_gather(block, axis), axis=0)]
    all_gather x0 -> x8, blocking collectives: none -> 69.4 us  [from_root(): return jnp.sum(lax.all_gather(block, axis), axis=0)]
    while x0 -> x8, blocking collectives: none -> 63.8 us
    psum x8 -> x0, blocking collectives: 62.1 us -> none  [from_root(): return lax.psum(block, axis)]
    reduce_sum x0 -> x24, other arithmetic: none -> 36.1 us  [from_root(): return jnp.sum(lax.all_gather(block, axis), axis=0)]
    while x0 -> x16, other arithmetic: none -> 11.6 us
    while x0 -> x16, local copies, waits for them, and re-layouts: none -> 10.5 us
  transfers between devices with their start and end apart: 12 -> 12, of which waited for: 11 -> 11; matrix products, arithmetic and copies ran while one was open for 20% -> 26% of each run, Pallas kernels for 0% -> 0%
where the time goes in v1:
time: 773 us; the launch traced here: 770 us
  waiting for transfers between devices  374 us (48%)
  blocking collectives  133 us (17%)
  other arithmetic  129 us (17%)
  local copies, waits for them, and re-layouts  84.8 us (11%)
  matrix products  33.2 us (4%)
  between operations  15.7 us (2%)
    all_gather x8, waiting for transfers between devices, from_root(): return jnp.sum(lax.all_gather(block, axis), axis=0)  216 us
    reduce_scatter x1, waiting for transfers between devices, body(): lax.psum_scatter(grad_part, 'narrow', scatter_dimension=0, tiled=True)  77.9 us
    all_gather x1, waiting for transfers between devices, body(): lax.all_gather(tokens, 'narrow', axis=0, tiled=True)  74.6 us
    all_gather x8, blocking collectives, from_root(): return jnp.sum(lax.all_gather(block, axis), axis=0)  69.4 us
    while x8, blocking collectives  63.8 us
    reduce_sum x24, other arithmetic, from_root(): return jnp.sum(lax.all_gather(block, axis), axis=0)  36.1 us
    scatter-add x4, other arithmetic, forward(): running.at[:, idx_second]  30.8 us
    scatter-add x4, other arithmetic, backward(): running.at[:, idx_first]  30.5 us
  transfers between devices with their start and end apart: 12, of which 11 were waited for; matrix products, arithmetic and copies ran while one was open for 26% of the time, Pallas kernels for 0%

profile of v1, /device:TPU:0, one launch (start us, length us, event | category | flops | bytes accessed | tf_op | source)
XLA Modules:
  0.0 770.2 jit_solution(9058113078050698652)
XLA Ops:
  10.3 430.7 %while.43 = (s32[]{:T(128)}, bf16[8,6,256,256]{3,2,1,0:T(8,128)(2,1)}, s32[8,6]{1,0:T(8,128)S(1)}, s32[8]{0:T(128)S(1)}, bf16[1,6,256,256]{3,2,1,0:T(8,128)(2,1)...) while((s32[]{:T(128)}, ...), condition=%wide.region_4.5_spmd, body=%wide.region_0.4_spmd.sunk | while | flops 3145800 | bytes 31458272 | solution.py:41
  15.8 7.6 all-reduce.2
  23.4 8.1 %all-gather.7 = s32[8,1,6]{2,1,0:T(1,128)S(1)} all-gather(s32[1,1,6]{2,1,0:T(1,128)S(1)} %fusion.101), channel_id=3, replica_groups=mesh['wide'=8,'narrow'=4] {'wide'}, dimensions={0}, use_global_device_ids=true | all-gather | bytes 216 | tf_op jit(solution)/shard_map/while/body/eval_jaxpr/all_gather | solution.py:9
  33.0 28.9 %all-gather.16.cloned.1.call-done = bf16[8,6,256,256]{3,2,1,0:T(8,128)(2,1)} async-done(((bf16[1,6,256,256]{3,2,1,0:T(8,128)(2,1)}), bf16[8,6,256,256]{3,2,1,0:T(8,128)(2,1)}) %all-gather.16.cloned.1.call-update) | async-done | bytes 6291472 | tf_op jit(solution)/shard_map/while/body/eval_jaxpr/all_gather | solution.py:9
  61.8 3.8 reduce.30
  70.2 7.1 all-reduce.2
  77.3 8.7 %all-gather.7 = s32[8,1,6]{2,1,0:T(1,128)S(1)} all-gather(s32[1,1,6]{2,1,0:T(1,128)S(1)} %fusion.101), channel_id=3, replica_groups=mesh['wide'=8,'narrow'=4] {'wide'}, dimensions={0}, use_global_device_ids=true | all-gather | bytes 216 | tf_op jit(solution)/shard_map/while/body/eval_jaxpr/all_gather | solution.py:9
  87.5 27.9 %all-gather.16.cloned.1.call-done = bf16[8,6,256,256]{3,2,1,0:T(8,128)(2,1)} async-done(((bf16[1,6,256,256]{3,2,1,0:T(8,128)(2,1)}), bf16[8,6,256,256]{3,2,1,0:T(8,128)(2,1)}) %all-gather.16.cloned.1.call-update) | async-done | bytes 6291472 | tf_op jit(solution)/shard_map/while/body/eval_jaxpr/all_gather | solution.py:9
  115.4 3.8 reduce.30
  123.8 8.0 %all-reduce.2 = s32[8]{0:T(128)S(1)} all-reduce(s32[8]{0:T(128)S(1)} %select_dynamic-update-slice_fusion.2), channel_id=4, replica_groups=mesh['wide'=8,'narrow'=4] {'wide'}, use_global_device_ids=true, to_apply=%add | all-reduce | flops 8 | bytes 64 | tf_op jit(solution)/shard_map/while
  131.8 9.5 %all-gather.7 = s32[8,1,6]{2,1,0:T(1,128)S(1)} all-gather(s32[1,1,6]{2,1,0:T(1,128)S(1)} %fusion.101), channel_id=3, replica_groups=mesh['wide'=8,'narrow'=4] {'wide'}, dimensions={0}, use_global_device_ids=true | all-gather | bytes 216 | tf_op jit(solution)/shard_map/while/body/eval_jaxpr/all_gather | solution.py:9
  142.8 26.2 %all-gather.16.cloned.1.call-done = bf16[8,6,256,256]{3,2,1,0:T(8,128)(2,1)} async-done(((bf16[1,6,256,256]{3,2,1,0:T(8,128)(2,1)}), bf16[8,6,256,256]{3,2,1,0:T(8,128)(2,1)}) %all-gather.16.cloned.1.call-update) | async-done | bytes 6291472 | tf_op jit(solution)/shard_map/while/body/eval_jaxpr/all_gather | solution.py:9
  169.0 3.8 reduce.30
  177.5 7.8 %all-reduce.2 = s32[8]{0:T(128)S(1)} all-reduce(s32[8]{0:T(128)S(1)} %select_dynamic-update-slice_fusion.2), channel_id=4, replica_groups=mesh['wide'=8,'narrow'=4] {'wide'}, use_global_device_ids=true, to_apply=%add | all-reduce | flops 8 | bytes 64 | tf_op jit(solution)/shard_map/while
  185.3 9.5 %all-gather.7 = s32[8,1,6]{2,1,0:T(1,128)S(1)} all-gather(s32[1,1,6]{2,1,0:T(1,128)S(1)} %fusion.101), channel_id=3, replica_groups=mesh['wide'=8,'narrow'=4] {'wide'}, dimensions={0}, use_global_device_ids=true | all-gather | bytes 216 | tf_op jit(solution)/shard_map/while/body/eval_jaxpr/all_gather | solution.py:9
  196.3 26.1 %all-gather.16.cloned.1.call-done = bf16[8,6,256,256]{3,2,1,0:T(8,128)(2,1)} async-done(((bf16[1,6,256,256]{3,2,1,0:T(8,128)(2,1)}), bf16[8,6,256,256]{3,2,1,0:T(8,128)(2,1)}) %all-gather.16.cloned.1.call-update) | async-done | bytes 6291472 | tf_op jit(solution)/shard_map/while/body/eval_jaxpr/all_gather | solution.py:9
  222.4 3.8 reduce.30
  230.9 8.9 %all-reduce.2 = s32[8]{0:T(128)S(1)} all-reduce(s32[8]{0:T(128)S(1)} %select_dynamic-update-slice_fusion.2), channel_id=4, replica_groups=mesh['wide'=8,'narrow'=4] {'wide'}, use_global_device_ids=true, to_apply=%add | all-reduce | flops 8 | bytes 64 | tf_op jit(solution)/shard_map/while
  239.7 8.4 %all-gather.7 = s32[8,1,6]{2,1,0:T(1,128)S(1)} all-gather(s32[1,1,6]{2,1,0:T(1,128)S(1)} %fusion.101), channel_id=3, replica_groups=mesh['wide'=8,'narrow'=4] {'wide'}, dimensions={0}, use_global_device_ids=true | all-gather | bytes 216 | tf_op jit(solution)/shard_map/while/body/eval_jaxpr/all_gather | solution.py:9
  249.6 26.1 %all-gather.16.cloned.1.call-done = bf16[8,6,256,256]{3,2,1,0:T(8,128)(2,1)} async-done(((bf16[1,6,256,256]{3,2,1,0:T(8,128)(2,1)}), bf16[8,6,256,256]{3,2,1,0:T(8,128)(2,1)}) %all-gather.16.cloned.1.call-update) | async-done | bytes 6291472 | tf_op jit(solution)/shard_map/while/body/eval_jaxpr/all_gather | solution.py:9
  275.7 3.8 reduce.30
  284.2 7.1 all-reduce.2
  291.3 9.9 %all-gather.7 = s32[8,1,6]{2,1,0:T(1,128)S(1)} all-gather(s32[1,1,6]{2,1,0:T(1,128)S(1)} %fusion.101), channel_id=3, replica_groups=mesh['wide'=8,'narrow'=4] {'wide'}, dimensions={0}, use_global_device_ids=true | all-gather | bytes 216 | tf_op jit(solution)/shard_map/while/body/eval_jaxpr/all_gather | solution.py:9
  302.7 26.4 %all-gather.16.cloned.1.call-done = bf16[8,6,256,256]{3,2,1,0:T(8,128)(2,1)} async-done(((bf16[1,6,256,256]{3,2,1,0:T(8,128)(2,1)}), bf16[8,6,256,256]{3,2,1,0:T(8,128)(2,1)}) %all-gather.16.cloned.1.call-update) | async-done | bytes 6291472 | tf_op jit(solution)/shard_map/while/body/eval_jaxpr/all_gather | solution.py:9
  329.0 3.8 reduce.30
  337.5 8.8 %all-reduce.2 = s32[8]{0:T(128)S(1)} all-reduce(s32[8]{0:T(128)S(1)} %select_dynamic-update-slice_fusion.2), channel_id=4, replica_groups=mesh['wide'=8,'narrow'=4] {'wide'}, use_global_device_ids=true, to_apply=%add | all-reduce | flops 8 | bytes 64 | tf_op jit(solution)/shard_map/while
  346.3 8.1 %all-gather.7 = s32[8,1,6]{2,1,0:T(1,128)S(1)} all-gather(s32[1,1,6]{2,1,0:T(1,128)S(1)} %fusion.101), channel_id=3, replica_groups=mesh['wide'=8,'narrow'=4] {'wide'}, dimensions={0}, use_global_device_ids=true | all-gather | bytes 216 | tf_op jit(solution)/shard_map/while/body/eval_jaxpr/all_gather | solution.py:9
  355.8 26.8 %all-gather.16.cloned.1.call-done = bf16[8,6,256,256]{3,2,1,0:T(8,128)(2,1)} async-done(((bf16[1,6,256,256]{3,2,1,0:T(8,128)(2,1)}), bf16[8,6,256,256]{3,2,1,0:T(8,128)(2,1)}) %all-gather.16.cloned.1.call-update) | async-done | bytes 6291472 | tf_op jit(solution)/shard_map/while/body/eval_jaxpr/all_gather | solution.py:9
  382.7 3.8 reduce.30
  391.1 8.6 %all-reduce.2 = s32[8]{0:T(128)S(1)} all-reduce(s32[8]{0:T(128)S(1)} %select_dynamic-update-slice_fusion.2), channel_id=4, replica_groups=mesh['wide'=8,'narrow'=4] {'wide'}, use_global_device_ids=true, to_apply=%add | all-reduce | flops 8 | bytes 64 | tf_op jit(solution)/shard_map/while
  399.7 7.2 all-gather.7
  408.3 28.0 %all-gather.16.cloned.1.call-done = bf16[8,6,256,256]{3,2,1,0:T(8,128)(2,1)} async-done(((bf16[1,6,256,256]{3,2,1,0:T(8,128)(2,1)}), bf16[8,6,256,256]{3,2,1,0:T(8,128)(2,1)}) %all-gather.16.cloned.1.call-update) | async-done | bytes 6291472 | tf_op jit(solution)/shard_map/while/body/eval_jaxpr/all_gather | solution.py:9
  436.3 3.8 reduce.30
  443.1 3.3 broadcast_multiply_fusion
  446.4 3.1 fusion.91
  449.5 74.6 %all-gather.12.cloned.1.call-done = bf16[512,4096]{0,1:T(8,128)(2,1)} async-done(((bf16[128,4096]{0,1:T(8,128)(2,1)}), bf16[512,4096]{0,1:T(8,128)(2,1)}) %all-gather.12.cloned.1.call-update) | async-done | bytes 4194320 | tf_op jit(solution)/shard_map/all_gather | solution.py:18
  524.1 6.4 copy.20
  530.4 4.1 broadcast_in_dim.36.clone
  534.5 59.7 %while.44 = (s32[]{:T(128)}, f32[512,16,256]{2,0,1:T(8,128)}, f32[4,512,256]{2,1,0:T(8,128)}, s32[4,6]{1,0:T(4,128)S(1)}, s32[4,6]{1,0:T(4,128)S(1)}, /*index=5*...) while((s32[]{:T(128)}, f32[512,16,256]{2,0,1:T(8,128)}, ...), condition=%wide.region_7.9_spmd, body=%wide.region_5.8_spmd.sunk | while | flops 808059968 | bytes 20452644 | solution.py:81
  534.5 2.9 gather_fusion
  541.8 7.7 %scatter_fusion = f32[512,16,256]{2,0,1:T(8,128)} fusion(f32[512,16,256]{2,0,1:T(8,128)} %get-tuple-element.624, s32[6]{0:T(128)S(1)} %fusion.104, f32[6,512,256]{2,1,0:T(8,128)S(1)} %convolution_bitcast_fusion.4), kind=kCustom, calls=%fused_computation.2.clone.1 | custom fusion | flops 786432 | bytes 9437208 | tf_op jit(solution)/shard_map/while/body/eval_jaxpr/scatter-add | solution.py:64
  549.6 2.9 gather_fusion
  556.8 7.7 %scatter_fusion = f32[512,16,256]{2,0,1:T(8,128)} fusion(f32[512,16,256]{2,0,1:T(8,128)} %get-tuple-element.624, s32[6]{0:T(128)S(1)} %fusion.104, f32[6,512,256]{2,1,0:T(8,128)S(1)} %convolution_bitcast_fusion.4), kind=kCustom, calls=%fused_computation.2.clone.1 | custom fusion | flops 786432 | bytes 9437208 | tf_op jit(solution)/shard_map/while/body/eval_jaxpr/scatter-add | solution.py:64
  571.7 7.7 scatter_fusion
  586.5 7.7 %scatter_fusion = f32[512,16,256]{2,0,1:T(8,128)} fusion(f32[512,16,256]{2,0,1:T(8,128)} %get-tuple-element.624, s32[6]{0:T(128)S(1)} %fusion.104, f32[6,512,256]{2,1,0:T(8,128)S(1)} %convolution_bitcast_fusion.4), kind=kCustom, calls=%fused_computation.2.clone.1 | custom fusion | flops 786432 | bytes 9437208 | tf_op jit(solution)/shard_map/while/body/eval_jaxpr/scatter-add | solution.py:64
  594.2 3.9 convert_bitcast_fusion.1
  600.7 4.0 all-gather.14.cloned.1.call-done
  604.7 6.4 copy.23
  611.1 4.1 broadcast_in_dim.36
  615.2 63.1 %while.45 = (s32[]{:T(128)}, f32[512,16,256]{2,0,1:T(8,128)}, s32[4,6]{1,0:T(4,128)S(1)}, s32[4,6]{1,0:T(4,128)S(1)}, bf16[512,16,256]{2,0,1:T(8,128)(2,1)}, /*i...) while((s32[]{:T(128)}, f32[512,16,256]{2,0,1:T(8,128)}, ...), condition=%wide.region_11.13_spmd, body=%wide.region_9.12_spmd.sunk | while | flops 809501760 | bytes 19404576 | solution.py:82
  615.2 4.1 gather_fusion.1
  619.3 4.0 convolution_bitcast_fusion.5
  623.3 7.6 scatter_fusion.1
  631.0 4.2 gather_fusion.1
  635.1 4.0 convolution_bitcast_fusion.5
  639.1 7.7 scatter_fusion.1
  646.8 4.1 gather_fusion.1
  650.9 4.1 convolution_bitcast_fusion.5
  654.9 7.6 scatter_fusion.1
  662.6 4.1 gather_fusion.1
  666.7 4.0 convolution_bitcast_fusion.5
  670.6 7.6 scatter_fusion.1
  678.2 3.9 convert_bitcast_fusion
  684.7 77.9 %reduce-scatter.5.cloned.1.call-done = bf16[128,4096]{1,0:T(8,128)(2,1)} async-done(((bf16[512,4096]{1,0:T(8,128)(2,1)}), bf16[128,4096]{1,0:T(8,128)(2,1)}) %reduce-scatter.5.cloned.1.call-update) | async-done | bytes 1048592 | tf_op jit(solution)/shard_map/reduce_scatter | solution.py:87
  (151 shorter events, 83.1 us)
Async XLA Ops:
  10.3 431.4 %copy-start = (bf16[128,4096]{1,0:T(8,128)(2,1)S(1)}, bf16[128,4096]{1,0:T(8,128)(2,1)}, u32[]{:S(2)}) copy-start(bf16[128,4096]{1,0:T(8,128)(2,1)} %param.14) | copy-start | bytes 3145732
  10.3 51.5 %all-gather.16.cloned.1.call-start = ((), (), s32[]{:S(2)}) async-start(), calls=%async_computation.6 | async-start | bytes 7077888 | tf_op jit(solution)/shard_map/while/body/eval_jaxpr/all_gather | solution.py:9
  66.6 48.9 %all-gather.16.cloned.1.call-start = ((), (), s32[]{:S(2)}) async-start(), calls=%async_computation.6 | async-start | bytes 7077888 | tf_op jit(solution)/shard_map/while/body/eval_jaxpr/all_gather | solution.py:9
  120.2 48.9 %all-gather.16.cloned.1.call-start = ((), (), s32[]{:S(2)}) async-start(), calls=%async_computation.6 | async-start | bytes 7077888 | tf_op jit(solution)/shard_map/while/body/eval_jaxpr/all_gather | solution.py:9
  173.8 48.5 %all-gather.16.cloned.1.call-start = ((), (), s32[]{:S(2)}) async-start(), calls=%async_computation.6 | async-start | bytes 7077888 | tf_op jit(solution)/shard_map/while/body/eval_jaxpr/all_gather | solution.py:9
  227.2 48.5 %all-gather.16.cloned.1.call-start = ((), (), s32[]{:S(2)}) async-start(), calls=%async_computation.6 | async-start | bytes 7077888 | tf_op jit(solution)/shard_map/while/body/eval_jaxpr/all_gather | solution.py:9
  280.5 48.5 %all-gather.16.cloned.1.call-start = ((), (), s32[]{:S(2)}) async-start(), calls=%async_computation.6 | async-start | bytes 7077888 | tf_op jit(solution)/shard_map/while/body/eval_jaxpr/all_gather | solution.py:9
  333.8 48.9 %all-gather.16.cloned.1.call-start = ((), (), s32[]{:S(2)}) async-start(), calls=%async_computation.6 | async-start | bytes 7077888 | tf_op jit(solution)/shard_map/while/body/eval_jaxpr/all_gather | solution.py:9
  387.4 48.9 %all-gather.16.cloned.1.call-start = ((), (), s32[]{:S(2)}) async-start(), calls=%async_computation.6 | async-start | bytes 7077888 | tf_op jit(solution)/shard_map/while/body/eval_jaxpr/all_gather | solution.py:9
  441.0 83.0 %all-gather.12.cloned.1.call-start = ((), (), s32[]{:S(2)}) async-start(), calls=%async_computation.2 | async-start | bytes 5242880 | tf_op jit(solution)/shard_map/all_gather | solution.py:18
  441.6 163.1 %all-gather.14.cloned.1.call-start = ((), (), s32[]{:S(2)}) async-start(), calls=%async_computation.4 | async-start | bytes 5242880 | tf_op jit(solution)/shard_map/all_gather | solution.py:19
  443.0 241.7 %reduce-scatter.3.cloned.1.call-start = ((), (), s32[]{:S(2)}) async-start(), calls=%async_computation.3 | async-start | bytes 5242880 | tf_op jit(solution)/shard_map/reduce_scatter | solution.py:86
  600.7 161.9 %reduce-scatter.5.cloned.1.call-start = ((), (), s32[]{:S(2)}) async-start(), calls=%async_computation.5 | async-start | bytes 5242880 | tf_op jit(solution)/shard_map/reduce_scatter | solution.py:87
Sparse Core Ops, SparseCore 0:
  13.6 48.2 all-gather.15
  69.9 45.5 all-gather.15
  123.5 45.5 all-gather.15
  176.8 45.5 all-gather.15
  230.2 45.5 all-gather.15
  283.5 45.5 all-gather.15
  337.1 45.5 all-gather.15
  390.7 45.5 all-gather.15
Sparse Core Ops, SparseCore 1:
  443.6 80.4 all-gather.11
  526.1 78.6 all-gather.13
  607.4 74.9 reduce-scatter.2
  685.4 77.2 reduce-scatter.4
